TPU v7x, 32 devices: a whole 2x2x4 slice. The times are simulated.
32 devices in a mesh: var: 4 (over x, core), space: 8 (over z, y).
Axes of the slice: x: 2, y: 2, z: 4, core: 2. Of those that a mesh axis runs over, the one named last changes fastest.
Arguments:
- fields: bfloat16 [8, 1024, 32768], P('var', None, 'space'), may hold values from -6 to 6
- eigenfunctions: bfloat16 [8, 64, 32768], P('var', None, 'space'), may hold values from -0.03125 to 0.03125
- start: float32 [512, 128], replicated, may hold values from -6 to 6
- grid_count: int32 [8], replicated, may hold values from 16384 to 32768
Outputs:
- loadings: bfloat16 [8, 128, 32768], P('var', None, 'space')
- component_scores: float32 [1024, 128], replicated
- explained: float32 [8, 1024], P('var')
Inputs may be any that keep to these rules, and one draw needn't show every extreme that they name: The grid of variable v is its points 0 to grid_count[v] - 1.
All inputs are finite; a program needn't handle non-finite values.
Results may differ from a plain program's by a relative error of at most 0.005.
Values sent between devices are 32-bit elements; how exact they have to be, the bound alone decides.
A program may use at most 64 MiB of HBM per device.

v0:
```python
import functools

import jax
import jax.numpy as jnp
from jax import lax
from jax.experimental import pallas as pl
from jax.experimental.pallas import tpu as pltpu
from jax.sharding import PartitionSpec as P

M = 64
SWEEPS = 2
MESH = pl.DeviceIdType.MESH
F32 = jnp.float32
BF16 = jnp.bfloat16
HIGHEST = lax.Precision.HIGHEST


def dot(left, right, dims, precision=None):
    return lax.dot_general(left, right, (dims, ((), ())), precision=precision, preferred_element_type=F32)


NN = ((1,), (0,))
NT = ((1,), (1,))
TN = ((0,), (0,))


def split(x):
    high = x.astype(BF16)
    return high, (x - high.astype(F32)).astype(BF16)


def dot3(left, right, dims):
    (lh, ll), (rh, rl) = left, right
    return dot(lh, rh, dims) + (dot(lh, rl, dims) + dot(ll, rh, dims))


def remote(src, dst, send, recv, target):
    return pltpu.make_async_remote_copy(
        src_ref=src, dst_ref=dst, send_sem=send, recv_sem=recv, device_id=target, device_id_type=MESH
    )


def masked_block(count, eigen, first):
    points = first + lax.broadcasted_iota(jnp.int32, (1, eigen.shape[1]), 1)
    return eigen * jnp.where(points < count, 1.0, 0.0).astype(eigen.dtype)


def gather_kernel(
    n, nv, counts, fields, eigen, centred_ref, gram_ref,
    fbuf, weights, part, rbuf, red, gpart, grbuf, gred, gfull, jbuf,
    fsem, asend, arecv, gsend, grecv, hsend, hrecv,
    zsend, zrecv, xsend, xrecv, ysend, yrecv, usend, urecv, wsend, wrecv, psend, precv,
):
    var, me = lax.axis_index("var"), lax.axis_index("space")
    local_vars, samples, local_points = fields.shape
    rows = samples // n
    width = local_vars * M
    half = rows // 2
    na, nz = nv // 2, n // 2
    side, core = var // 2, lax.rem(var, 2)
    depth, lane_y = me // 2, lax.rem(me, 2)
    partner = 2 * side + 1 - core

    def at(i):
        return 2 * lax.rem(depth + 1 + i // 2, nz) + lax.rem(lane_y + 1 + lax.rem(i, 2), 2)

    def fetch(i):
        block = pl.ds(pl.multiple_of(at(i) * rows, rows), rows)
        slot = lax.rem(i, 3)
        return pltpu.make_async_copy(fields.at[:, block, :], fbuf.at[slot], fsem.at[slot])

    fetch(0).start()
    fetch(1).start()

    barrier = pltpu.get_barrier_semaphore()
    for d in range(1, n):
        pl.semaphore_signal(barrier, inc=1, device_id=(var, lax.rem(me + d, n)), device_id_type=MESH)
    for d in range(1, nv):
        pl.semaphore_signal(barrier, inc=1, device_id=(lax.rem(var + d, nv), me), device_id_type=MESH)

    grams = []
    for v in range(local_vars):
        masked = masked_block(counts[var * local_vars + v], eigen[v], me * local_points)
        grams.append(dot(masked, masked, NT))
        weights[:, v * M:(v + 1) * M] = masked.T
    gram = jnp.concatenate(grams, axis=1)
    grows = M // n
    gpart[...] = jnp.zeros_like(gpart)
    for s in range(n):
        gpart[s, 0:grows, :] = gram[s * grows:(s + 1) * grows, :]

    pl.semaphore_wait(barrier, n - 1 + nv - 1)

    def send_part(i):
        return remote(part.at[i], rbuf.at[i], asend.at[i], arecv.at[i], (var, at(i)))

    def send_gram(i):
        return remote(gpart.at[at(i)], grbuf.at[i], gsend.at[i], grecv.at[i], (var, at(i)))

    owner = lax.broadcasted_iota(jnp.int32, (rows, width), 1) // M

    def step(i, carry):
        slot = lax.rem(i, 3)

        @pl.when(i + 2 < n)
        def _():
            fetch(i + 2).start()

        @pl.when(i > 0)
        def _():
            send_part(i - 1).start()
            send_gram(i - 1).start()

        fetch(i).wait()
        scores = dot(fbuf[slot, 0], weights[...], NN)
        for v in range(1, local_vars):
            scores = jnp.where(owner == v, dot(fbuf[slot, v], weights[...], NN), scores)
        part[i] = scores
        return carry

    lax.fori_loop(0, n, step, 0)

    def wait_part(i, carry):
        send_part(i).wait()
        send_gram(i).wait()
        return carry

    lax.fori_loop(0, n - 1, wait_part, 0)

    def block(a, z, y, low=0, size=rows):
        return jbuf.at[
            pl.ds(pl.multiple_of((2 * z + y) * rows + low, size), size),
            pl.ds(pl.multiple_of((2 * a + core) * width, width), width),
        ]

    total = part[n - 1]
    gtotal = gpart[me]
    for i in range(n - 1):
        total = total + rbuf[i]
        gtotal = gtotal + grbuf[i]
    red[...] = total
    gred[...] = gtotal
    block(side, depth, lane_y)[...] = total
    gfull[me] = gtotal

    def from_depth(t):
        return lax.rem(depth - t + nz, nz)

    def send_gfull(d):
        return remote(gred, gfull.at[me], hsend.at[d - 1], hrecv.at[d - 1], (var, lax.rem(me + d, n)))

    def send_z(t):
        target = (var, 2 * lax.rem(depth + t, nz) + lane_y)
        return remote(red, block(side, depth, lane_y), zsend.at[t - 1], zrecv.at[t - 1], target)

    def other(e):
        return lax.rem(side + e, na)

    def back(e):
        return lax.rem(side - e + na, na)

    beside = 1 - lane_y

    def send_x(t, e):
        mine = block(side, from_depth(t), lane_y)
        j = t * (na - 1) + e - 1
        return remote(red if t == 0 else mine, mine, xsend.at[j], xrecv.at[j], (2 * other(e) + core, me))

    def send_y(t):
        mine = block(side, from_depth(t), lane_y)
        return remote(red if t == 0 else mine, mine, ysend.at[t], yrecv.at[t], (var, 2 * depth + beside))

    def relay_y(t, e):
        piece = block(back(e), from_depth(t), lane_y, 0, half)
        j = t * (na - 1) + e - 1
        return remote(piece, piece, usend.at[j], urecv.at[j], (var, 2 * depth + beside))

    def relay_x(t, e):
        piece = block(side, from_depth(t), beside, half, half)
        j = t * (na - 1) + e - 1
        return remote(piece, piece, wsend.at[j], wrecv.at[j], (2 * other(e) + core, me))

    def to_partner(t, e, y):
        piece = block(back(e), from_depth(t), lane_y if y == 0 else beside)
        j = (t * na + e) * 2 + y
        return remote(piece, piece, psend.at[j], precv.at[j], (partner, me))

    for t in range(1, nz):
        send_z(t).start()
    for s in range(nz + 2):
        if s < nz:
            if s > 0:
                send_z(s).wait_recv()
            for e in range(1, na):
                send_x(s, e).start()
            send_y(s).start()
            to_partner(s, 0, 0).start()
            if s == 0:
                for d in range(1, n):
                    send_gfull(d).start()
        if 0 <= s - 1 < nz:
            for e in range(1, na):
                send_x(s - 1, e).wait_recv()
                relay_y(s - 1, e).start()
                to_partner(s - 1, e, 0).start()
            send_y(s - 1).wait_recv()
            for e in range(1, na):
                relay_x(s - 1, e).start()
            to_partner(s - 1, 0, 1).start()
        if 0 <= s - 2 < nz:
            for e in range(1, na):
                relay_y(s - 2, e).wait_recv()
                relay_x(s - 2, e).wait_recv()
                to_partner(s - 2, e, 1).start()
    for d in range(1, n):
        send_gfull(d).wait()
    for t in range(1, nz):
        send_z(t).wait_send()
    for t in range(nz):
        send_y(t).wait_send()
        for e in range(1, na):
            send_x(t, e).wait_send()
            relay_y(t, e).wait_send()
            relay_x(t, e).wait_send()
        for e in range(na):
            for y in range(2):
                to_partner(t, e, y).wait()

    mean = jnp.sum(jbuf[...], axis=0, keepdims=True) / samples
    centred_ref[...] = jbuf[...] - mean
    for s in range(n):
        gram_ref[s * grows:(s + 1) * grows, :] = gfull[s, 0:grows, :]


def gather_scores(n, nv, counts, fields, eigen):
    local_vars, samples, points = fields.shape
    rows = samples // n
    width = local_vars * M
    na, nz = nv // 2, n // 2
    dma = pltpu.SemaphoreType.DMA
    pairs = [n - 1, n - 1, n - 1, nz - 1, nz * (na - 1), nz, nz * (na - 1), nz * (na - 1), 2 * nz * na]
    return pl.pallas_call(
        functools.partial(gather_kernel, n, nv),
        out_shape=(
            jax.ShapeDtypeStruct((samples, nv * width), F32),
            jax.ShapeDtypeStruct((M, width), F32),
        ),
        in_specs=[
            pl.BlockSpec(memory_space=pltpu.SMEM),
            pl.BlockSpec(memory_space=pl.ANY),
            pl.BlockSpec(memory_space=pltpu.VMEM),
        ],
        out_specs=(pl.BlockSpec(memory_space=pltpu.VMEM), pl.BlockSpec(memory_space=pltpu.VMEM)),
        scratch_shapes=[
            pltpu.VMEM((3, local_vars, rows, points), BF16),
            pltpu.VMEM((points, width), BF16),
            pltpu.VMEM((n, rows, width), F32),
            pltpu.VMEM((n - 1, rows, width), F32),
            pltpu.VMEM((rows, width), F32),
            pltpu.VMEM((n, 8, width), F32),
            pltpu.VMEM((n - 1, 8, width), F32),
            pltpu.VMEM((8, width), F32),
            pltpu.VMEM((n, 8, width), F32),
            pltpu.VMEM((samples, nv * width), F32),
            dma((3,)),
            *[dma((count,)) for count in pairs for _ in range(2)],
        ],
        compiler_params=pltpu.CompilerParams(
            collective_id=0, has_side_effects=True, vmem_limit_bytes=48 * 1024 * 1024
        ),
        name="gather_scores",
    )(counts, fields, eigen)


def inverse_factor(gram):
    size = gram.shape[0]
    tiles = size // 8
    rows = [gram[8 * i:8 * i + 8, :] for i in range(tiles)]
    lane = lax.broadcasted_iota(jnp.int32, (8, size), 1)
    sublane = lax.broadcasted_iota(jnp.int32, (8, size), 0)

    def column(tile, k):
        return jnp.broadcast_to(tile[:, k:k + 1], (8, size))

    def spread(tile, j):
        return jnp.broadcast_to(tile[j:j + 1, :], (8, size))

    done = []
    for b in range(tiles):
        base = 8 * b
        inside = (lane >= base) & (lane < base + 8)
        tops = [column(rows[b], base + j) for j in range(8)]
        entry = {(i, j): spread(tops[j], i) for j in range(8) for i in range(j, 8)}
        unit = jnp.where(inside, jnp.where(lane - base == sublane, 1.0, 0.0), rows[b])
        line = [spread(unit, j) for j in range(8)]
        inverse = []
        for j in range(8):
            inverse.append(1.0 / entry[j, j])
            for i in range(j + 1, 8):
                factor = entry[i, j] * inverse[j]
                for q in range(j + 1, i + 1):
                    entry[i, q] = entry[i, q] - factor * entry[q, j]
                line[i] = line[i] - factor * line[j]
        rest = line[0]
        pivot = entry[0, 0]
        for j in range(1, 8):
            rest = jnp.where(sublane == j, line[j], rest)
            pivot = jnp.where(sublane == j, entry[j, j], pivot)
        done.append(jnp.where(lane < base + 8, rest, 0.0) * lax.rsqrt(pivot))
        for i in range(b + 1, tiles):
            new = jnp.where(inside, 0.0, rows[i])
            factors = []
            for j in range(8):
                value = column(rows[i], base + j)
                for p in range(j):
                    value = value - factors[p] * entry[j, p]
                factors.append(value * inverse[j])
            for j in range(8):
                new = new - factors[j] * line[j]
            rows[i] = new
    return done


def basis_kernel(
    counts, centred_ref, gram_ref, start_ref, eigen_ref, loadings_ref, scores_ref, explained_ref,
    high_ref, low_ref, cov_high, cov_low, basis_ref, inverse_ref,
):
    var = lax.axis_index("var")
    samples = centred_ref.shape[0]
    local_vars = eigen_ref.shape[0]
    first_point = lax.axis_index("space") * eigen_ref.shape[2]
    width = local_vars * M
    high, low = split(centred_ref[...])
    high_ref[...] = high
    low_ref[...] = low
    cov = dot3((high, low), (high, low), TN) / (samples - 1)
    cov_high[...], cov_low[...] = split(cov)
    basis_ref[...] = start_ref[...]

    def sweep(_, carry):
        image = dot3((cov_high[...], cov_low[...]), split(basis_ref[...]), NN)
        gram = dot(image, image, TN, HIGHEST)
        for i, tile in enumerate(inverse_factor(gram)):
            inverse_ref[8 * i:8 * i + 8, :] = tile
        basis_ref[...] = dot(image, inverse_ref[...], NT, HIGHEST)
        return carry

    lax.fori_loop(0, SWEEPS, sweep, 0)

    scores = dot3((high_ref[...], low_ref[...]), split(basis_ref[...]), NN)
    scores_ref[...] = scores
    scores_low = scores.astype(BF16)
    own = pl.ds(pl.multiple_of(var * width, width), width)
    basis_low = basis_ref[own, :].astype(BF16)
    own_high, own_low = high_ref[:, own], low_ref[:, own]
    ones = jnp.ones((8, basis_low.shape[1]), F32)
    scores_wide = scores_low.astype(F32)
    for v in range(local_vars):
        mine = basis_low[v * M:(v + 1) * M, :]
        masked = masked_block(counts[var * local_vars + v], eigen_ref[v], first_point)
        loadings_ref[v] = dot(mine, masked, TN).astype(BF16)
        left, right = own_high[:, v * M:(v + 1) * M], own_low[:, v * M:(v + 1) * M]
        cross = dot(left, mine, NN) + dot(right, mine, NN)
        wide = mine.astype(F32)
        inner = dot(gram_ref[:, v * M:(v + 1) * M], wide, NN, HIGHEST)
        square = split(dot(wide, inner, TN, HIGHEST))
        quad = dot(scores_low, square[0], NN) + dot(scores_low, square[1], NN)
        gain = scores_wide * (2.0 * cross - quad)
        summed = dot(ones, gain, NT, HIGHEST) / M
        explained_ref[v:v + 1, :] = summed[0:1, :]


def finish(counts, centred, gram, start, eigen):
    local_vars, _, points = eigen.shape
    samples, joint = centred.shape
    k = start.shape[1]
    return pl.pallas_call(
        basis_kernel,
        out_shape=(
            jax.ShapeDtypeStruct((local_vars, k, points), BF16),
            jax.ShapeDtypeStruct((samples, k), F32),
            jax.ShapeDtypeStruct((local_vars, samples), F32),
        ),
        in_specs=[pl.BlockSpec(memory_space=pltpu.SMEM)] + [pl.BlockSpec(memory_space=pltpu.VMEM)] * 4,
        out_specs=(pl.BlockSpec(memory_space=pltpu.VMEM),) * 3,
        scratch_shapes=[
            pltpu.VMEM((samples, joint), BF16),
            pltpu.VMEM((samples, joint), BF16),
            pltpu.VMEM((joint, joint), BF16),
            pltpu.VMEM((joint, joint), BF16),
            pltpu.VMEM((joint, k), F32),
            pltpu.VMEM((k, k), F32),
        ],
        compiler_params=pltpu.CompilerParams(vmem_limit_bytes=48 * 1024 * 1024),
        name="finish",
    )(counts, centred, gram, start, eigen)


def shards(n, nv, fields, eigenfunctions, start, grid_count):
    centred, gram = gather_scores(n, nv, grid_count, fields, eigenfunctions)
    return finish(grid_count, centred, gram, start, eigenfunctions)


def solution(mesh):
    return jax.shard_map(
        functools.partial(shards, mesh.shape["space"], mesh.shape["var"]),
        mesh=mesh,
        in_specs=(P("var", None, "space"), P("var", None, "space"), P(), P()),
        out_specs=(P("var", None, "space"), P(), P("var", None)),
        check_vma=False,
    )
```

profile of v0, /device:TPU:0, one launch (start us, length us, event | category | flops | bytes accessed | tf_op | source)
XLA Modules:
  0.0 61.7 jit_solution(6792998921546239655)
XLA Ops:
  0.6 0.0 copy-start
  0.6 1.2 %copy-done = bf16[2,64,4096]{2,1,0:T(8,128)(2,1)S(1)} copy-done((bf16[2,64,4096]{2,1,0:T(8,128)(2,1)S(1)}, bf16[2,64,4096]{2,1,0:T(8,128)(2,1)}, u32[]{:S(2)}) %copy-start) | copy-done | bytes 1048600
  1.9 0.0 copy-start.2
  1.9 0.7 %copy-done.2 = s32[8]{0:T(128)S(1)} copy-done((s32[8]{0:T(128)S(1)}, s32[8]{0:T(128)}, u32[]{:S(2)}) %copy-start.2) | copy-done | bytes 56
  2.5 0.0 copy-start.1
  2.5 39.0 %gather_scores.1 = (f32[1024,512]{1,0:T(8,128)S(1)}, f32[64,128]{1,0:T(8,128)S(1)}) custom-call(s32[8]{0:T(128)S(1)} %copy-done.2, bf16[2,1024,4096]{2,1,0:T(8,128)(2,1)} %fields.1, bf16[2,64,4096]{2,1,0:T(8,128)(2,1)S(1)} %copy-done), custom_call_target="tpu_custom_call" | custom-call | tf_op jit(solution)/shard_map/gather_scores/pallas_call | solution.py:242
  41.6 0.0 copy-done.1
  41.6 20.1 %finish.1 = (bf16[2,128,4096]{2,1,0:T(8,128)(2,1)}, f32[1024,128]{1,0:T(8,128)}, f32[2,1024]{1,0:T(2,128)}) custom-call(s32[8]{0:T(128)S(1)} %copy-done.2, f32[1024,512]{1,0:T(8,128)S(1)} %get-tuple-element.5.centred_ref, f32[64,128]{1,0:T(8,128)S(1)} %get-tuple-element.6.gram_ref, f32[512,128]{1,0:T(8,128)S(1)} %copy-done.1, bf16[2,64,4096]{2,1,0:T(8,128)(2,1)S(1)} %copy-done), custom_call_target="tpu_custom_call" | custom-call | tf_op jit(solution)/shard_map/finish/pallas_call | solution.py:377
Async XLA Ops:
  0.6 1.2 %copy-start = (bf16[2,64,4096]{2,1,0:T(8,128)(2,1)S(1)}, bf16[2,64,4096]{2,1,0:T(8,128)(2,1)}, u32[]{:S(2)}) copy-start(bf16[2,64,4096]{2,1,0:T(8,128)(2,1)} %eigen_ref.1) | copy-start | bytes 3145732
  1.9 0.7 %copy-start.2 = (s32[8]{0:T(128)S(1)}, s32[8]{0:T(128)}, u32[]{:S(2)}) copy-start(s32[8]{0:T(128)} %counts.3) | copy-start | bytes 100
  2.5 39.1 %copy-start.1 = (f32[512,128]{1,0:T(8,128)S(1)}, f32[512,128]{1,0:T(8,128)}, u32[]{:S(2)}) copy-start(f32[512,128]{1,0:T(8,128)} %start_ref.1) | copy-start | bytes 786436
where the time goes:
time: 61.9 us; the launch traced here: 61.7 us
  Pallas kernels  59.1 us (95%)
  local copies, waits for them, and re-layouts  1.88 us (3%)
  between operations  0.66 us (1%)
    pallas_call x1, Pallas kernels, gather_scores(): pl.pallas_call(functools.partial(gather_kernel, n, nv), out_shape=(jax.Sh...  39 us
    pallas_call x1, Pallas kernels, finish(): pl.pallas_call(basis_kernel, out_shape=(jax.ShapeDtypeStruct((local_vars,...  20.1 us
    unnamed x6, local copies, waits for them, and re-layouts  1.88 us

commit v1 on v0

v1 whole, which is shorter than its diff:
```python
import functools

import jax
import jax.numpy as jnp
from jax import lax
from jax.experimental import pallas as pl
from jax.experimental.pallas import tpu as pltpu
from jax.sharding import PartitionSpec as P

M = 64
SWEEPS = 2
MESH = pl.DeviceIdType.MESH
F32 = jnp.float32
BF16 = jnp.bfloat16
HIGHEST = lax.Precision.HIGHEST


def dot(left, right, dims, precision=None):
    return lax.dot_general(left, right, (dims, ((), ())), precision=precision, preferred_element_type=F32)


NN = ((1,), (0,))
NT = ((1,), (1,))
TN = ((0,), (0,))


def split(x):
    high = x.astype(BF16)
    return high, (x - high.astype(F32)).astype(BF16)


def dot3(left, right, dims):
    (lh, ll), (rh, rl) = left, right
    return dot(lh, rh, dims) + (dot(lh, rl, dims) + dot(ll, rh, dims))


def remote(src, dst, send, recv, target):
    return pltpu.make_async_remote_copy(
        src_ref=src, dst_ref=dst, send_sem=send, recv_sem=recv, device_id=target, device_id_type=MESH
    )


def masked_block(count, eigen, first):
    points = first + lax.broadcasted_iota(jnp.int32, (1, eigen.shape[1]), 1)
    return eigen * jnp.where(points < count, 1.0, 0.0).astype(eigen.dtype)


def gather_kernel(
    n, pieces, counts_hbm, fields, eigen_hbm, centred_ref, gram_ref, masked_ref,
    counts, eigen, fbuf, weights, part, rbuf, cross, jbuf, gpart, grbuf, gred, gfull,
    csem, esem, fsem, rsend, rrecv, xsend, xrecv, asend, arecv, psend, precv, gsend, grecv, hsend, hrecv,
):
    var, me = lax.axis_index("var"), lax.axis_index("space")
    local_vars, samples, local_points = fields.shape
    rows = samples // (4 * pieces)
    width = local_vars * M
    groups = n // 4
    side, core = var // 2, lax.rem(var, 2)
    group, quad = me // 4, lax.rem(me, 4)
    depth, lane_y = quad // 2, lax.rem(quad, 2)
    far, mate = 1 - side, 1 - core

    def owner(dz, dy):
        return 2 * (depth + dz - 2 * depth * dz) + lane_y + dy - 2 * lane_y * dy

    def fetch(i):
        first = (4 * (i // 2) + 2 * (owner(1 - lax.rem(i, 2), 0) // 2)) * rows
        block = pl.ds(pl.multiple_of(first, 2 * rows), 2 * rows)
        return pltpu.make_async_copy(fields.at[:, block, :], fbuf.at[i], fsem.at[i])

    eigen_copy = pltpu.make_async_copy(eigen_hbm, eigen, esem)
    counts_copy = pltpu.make_async_copy(counts_hbm, counts, csem)
    counts_copy.start()
    eigen_copy.start()
    lax.fori_loop(0, 2 * pieces, lambda i, carry: (fetch(i).start(), carry)[1], 0)

    xside, yside, zside = (2 * far + mate, me), (2 * side + mate, 4 * group + owner(0, 1)), (2 * side + mate, 4 * group + owner(1, 0))
    corner, partner = (2 * far + mate, 4 * group + owner(1, 1)), (2 * side + mate, me)
    barrier = pltpu.get_barrier_semaphore()
    for d in range(1, n):
        pl.semaphore_signal(barrier, inc=1, device_id=(var, lax.rem(me + d, n)), device_id_type=MESH)
    for target in (xside, yside, zside, corner, partner):
        pl.semaphore_signal(barrier, inc=1, device_id=target, device_id_type=MESH)

    counts_copy.wait()
    eigen_copy.wait()
    for v in range(local_vars):
        masked = masked_block(counts[var * local_vars + v], eigen[v], me * local_points)
        masked_ref[v] = masked
        weights[:, v * M:(v + 1) * M] = masked.T

    pl.semaphore_wait(barrier, n - 1 + 5)

    def send_part(p, k):
        j = 3 * p + k
        source = part.at[2 * p + k // 2, 1 - lane_y if k % 2 == 0 else lane_y]
        target = (var, 4 * group + owner(1 - k // 2, 1 - k % 2))
        return remote(source, rbuf.at[j], rsend.at[j], rrecv.at[j], target)

    column = lax.broadcasted_iota(jnp.int32, (2 * rows, width), 1) // M

    def project(i):
        fetch(i).wait()
        scores = dot(fbuf[i, 0], weights[...], NN)
        for v in range(1, local_vars):
            scores = jnp.where(column == v, dot(fbuf[i, v], weights[...], NN), scores)
        part[i, 0] = scores[0:rows]
        part[i, 1] = scores[rows:2 * rows]

    def step(p, carry):
        @pl.when(p > 0)
        def _():
            send_part(p - 1, 2).start()

        project(2 * p)
        send_part(p, 0).start()
        send_part(p, 1).start()
        project(2 * p + 1)
        return carry

    def block(p, origin, o):
        return jbuf.at[origin, pl.ds(pl.multiple_of((4 * p + o) * rows, rows), rows)]

    own = [block(p, var, quad) for p in range(pieces)]

    def send_cross(p, d):
        j = p * (groups - 1) + d - 1
        target = (var, 4 * lax.rem(group + d, groups) + quad)
        return remote(cross.at[p, group], cross.at[p, group], xsend.at[j], xrecv.at[j], target)

    def half_sum(p):
        total = part[2 * p + 1, lane_y]
        for k in range(3):
            send_part(p, k).wait_recv()
            total = total + rbuf[3 * p + k]
        cross[p, group] = total
        for d in range(1, groups):
            send_cross(p, d).start()

    def relation(p, kind):
        return {
            "x": lambda: block(p, 2 * far + mate, quad),
            "y": lambda: block(p, 2 * side + mate, owner(0, 1)),
            "z": lambda: block(p, 2 * side + mate, owner(1, 0)),
            "xy": lambda: block(p, 2 * far + core, owner(0, 1)),
            "xz": lambda: block(p, 2 * far + core, owner(1, 0)),
            "yz": lambda: block(p, 2 * side + core, owner(1, 1)),
            "xyz": lambda: block(p, 2 * far + mate, owner(1, 1)),
        }[kind]()

    kinds = ("x", "y", "z", "xy", "xz", "yz", "xyz")

    def route(p, kind):
        last = (("xyz", "yz", xside), ("xyz", "xz", yside), ("xyz", "xy", zside))[p % 3]
        if p == pieces - 1:
            last = ("xyz", "", corner)
        return {
            "x": ("", xside), "y": ("", yside), "z": ("", zside),
            "xz": ("x", zside), "xy": ("y", xside), "yz": ("z", yside), "xyz": last[1:],
        }[kind]

    def send_on(p, kind):
        source, target = route(p, kind)
        piece = own[p] if source == "" else relation(p, source)
        j = p * 7 + kinds.index(kind)
        return remote(piece, piece, asend.at[j], arecv.at[j], target)

    def share(p, kind):
        piece = own[p] if kind == "" else relation(p, kind)
        j = p * 8 + (7 if kind == "" else kinds.index(kind))
        return remote(piece, piece, psend.at[j], precv.at[j], partner)

    def arrived(p, kind):
        send_on(p, kind).wait_recv()
        for other in kinds:
            if route(p, other)[0] == kind:
                send_on(p, other).start()
        share(p, kind).start()

    def full_sum(p):
        for d in range(1, groups):
            send_cross(p, d).wait_recv()
        total = cross[p, 0]
        for g in range(1, groups):
            total = total + cross[p, g]
        own[p][...] = total
        for kind in kinds:
            if route(p, kind)[0] == "":
                send_on(p, kind).start()
        share(p, "").start()

    def first_hop(p):
        for kind in ("x", "y", "z"):
            arrived(p, kind)

    def second_hop(p):
        for kind in ("xy", "xz", "yz"):
            arrived(p, kind)

    def third_hop(p):
        arrived(p, "xyz")

    grows = M // n

    def send_gram(d):
        target = lax.rem(me + d, n)
        return remote(gpart.at[target], grbuf.at[d - 1], gsend.at[d - 1], grecv.at[d - 1], (var, target))

    def send_gfull(d):
        return remote(gred, gfull.at[me], hsend.at[d - 1], hrecv.at[d - 1], (var, lax.rem(me + d, n)))

    def gram_parts():
        grams = [dot(masked_ref[v], masked_ref[v], NT) for v in range(local_vars)]
        gram = jnp.concatenate(grams, axis=1)
        gpart[...] = jnp.zeros_like(gpart)
        for s in range(n):
            gpart[s, 0:grows, :] = gram[s * grows:(s + 1) * grows, :]
        for d in range(1, n):
            send_gram(d).start()

    def gram_sum():
        gtotal = gpart[me]
        for d in range(1, n):
            send_gram(d).wait()
            gtotal = gtotal + grbuf[d - 1]
        gred[...] = gtotal
        gfull[me] = gtotal
        for d in range(1, n):
            send_gfull(d).start()

    stages = (half_sum, full_sum, first_hop, second_hop, third_hop)
    early = max(pieces - 1, 1)
    lax.fori_loop(0, early, step, 0)
    half_sum(0)
    lax.fori_loop(early, pieces, step, 0)
    send_part(pieces - 1, 2).start()
    gram_parts()
    slots = sorted((1.5 * p + (0, 2.2, 3.8, 5.4, 7.0)[s], s, p) for s in range(5) for p in range(pieces))
    for at, s, p in slots[1:]:
        if (s, p) == (2, pieces - 1):
            gram_sum()
        stages[s](p)

    for d in range(1, n):
        send_gfull(d).wait()
    for p in range(pieces):
        for k in range(3):
            send_part(p, k).wait_send()
        for d in range(1, groups):
            send_cross(p, d).wait_send()
        for kind in kinds:
            send_on(p, kind).wait_send()
        for kind in kinds + ("",):
            share(p, kind).wait()

    for v in range(2 * (jbuf.shape[0] // 2)):
        mean = jnp.sum(jbuf[v], axis=0, keepdims=True) / samples
        centred_ref[:, v * width:(v + 1) * width] = jbuf[v] - mean
    for s in range(n):
        gram_ref[s * grows:(s + 1) * grows, :] = gfull[s, 0:grows, :]


def gather_scores(n, nv, counts, fields, eigen):
    local_vars, samples, points = fields.shape
    pieces = 4
    if nv != 4 or n % 4 or samples % (4 * pieces):
        raise ValueError("unsupported mesh")
    rows = samples // (4 * pieces)
    width = local_vars * M
    groups = n // 4
    dma = pltpu.SemaphoreType.DMA
    pairs = [3 * pieces, max(1, pieces * (groups - 1)), 7 * pieces, 8 * pieces, n - 1, n - 1]
    return pl.pallas_call(
        functools.partial(gather_kernel, n, pieces),
        out_shape=(
            jax.ShapeDtypeStruct((samples, nv * width), F32),
            jax.ShapeDtypeStruct((M, width), F32),
            jax.ShapeDtypeStruct((local_vars, M, points), BF16),
        ),
        in_specs=[pl.BlockSpec(memory_space=pltpu.HBM)] * 3,
        out_specs=(pl.BlockSpec(memory_space=pltpu.VMEM),) * 3,
        scratch_shapes=[
            pltpu.SMEM(counts.shape, jnp.int32),
            pltpu.VMEM((local_vars, M, points), BF16),
            pltpu.VMEM((2 * pieces, local_vars, 2 * rows, points), BF16),
            pltpu.VMEM((points, width), BF16),
            pltpu.VMEM((2 * pieces, 2, rows, width), F32),
            pltpu.VMEM((3 * pieces, rows, width), F32),
            pltpu.VMEM((pieces, groups, rows, width), F32),
            pltpu.VMEM((nv, samples, width), F32),
            pltpu.VMEM((n, 8, width), F32),
            pltpu.VMEM((n - 1, 8, width), F32),
            pltpu.VMEM((8, width), F32),
            pltpu.VMEM((n, 8, width), F32),
            dma(()),
            dma(()),
            dma((2 * pieces,)),
            *[dma((count,)) for count in pairs for _ in range(2)],
        ],
        compiler_params=pltpu.CompilerParams(
            collective_id=0, has_side_effects=True, vmem_limit_bytes=48 * 1024 * 1024
        ),
        name="gather_scores",
    )(*(pltpu.with_memory_space_constraint(x, pltpu.HBM) for x in (counts, fields, eigen)))


def inverse_factor(gram):
    size = gram.shape[0]
    tiles = size // 8
    rows = [gram[8 * i:8 * i + 8, :] for i in range(tiles)]
    lane = lax.broadcasted_iota(jnp.int32, (8, size), 1)
    sublane = lax.broadcasted_iota(jnp.int32, (8, size), 0)

    def columns(tile, b):
        return [jnp.broadcast_to(tile[:, 8 * b + j:8 * b + j + 1], (8, size)) for j in range(8)]

    def spread(tile, j):
        return jnp.broadcast_to(tile[j:j + 1, :], (8, size))

    done = []
    block = columns(rows[0], 0)
    for b in range(tiles):
        inside = (lane >= 8 * b) & (lane < 8 * b + 8)
        work = jnp.where(inside, jnp.where(lane - 8 * b == sublane, 1.0, 0.0), rows[b])
        inverse, cross, lower = [], {}, []
        pivot = None
        for j in range(8):
            diagonal = spread(block[j], j)
            pivot = diagonal if j == 0 else jnp.where(sublane == j, diagonal, pivot)
            inverse.append(1.0 / diagonal)
            for q in range(j + 1, 8):
                cross[j, q] = spread(block[j], q)
            if j == 7:
                break
            block[j + 1] = block[j + 1] - (block[j] * cross[j, j + 1]) * inverse[j]
            factor = block[j] * inverse[j]
            lower.append(factor)
            for q in range(j + 2, 8):
                block[q] = block[q] - factor * cross[j, q]
            work = work - jnp.where(sublane > j, factor, 0.0) * spread(work, j)
        done.append(jnp.where(lane < 8 * b + 8, work, 0.0) * lax.rsqrt(pivot))
        if b + 1 == tiles:
            break
        line = [spread(work, j) for j in range(8)]
        for i in range(b + 1, min(b + 3, tiles)):
            value, factors = columns(rows[i], b), []
            for j in range(8):
                factors.append(value[j] * inverse[j])
                for q in range(j + 1, 8):
                    value[q] = value[q] - factors[j] * cross[j, q]
            if i == b + 1:
                block = columns(rows[i], i)
                for q in range(8):
                    for j in range(8):
                        block[q] = block[q] - factors[j] * spread(value[j], q)
            new = jnp.where(inside, 0.0, rows[i])
            for j in range(8):
                new = new - factors[j] * line[j]
            rows[i] = new
        if b + 3 >= tiles:
            continue
        solved = [None] * 8
        for j in reversed(range(8)):
            value = line[j] * inverse[j]
            for q in range(j + 1, 8):
                value = value - spread(lower[j], q) * solved[q]
            solved[j] = value
        for i in range(b + 3, tiles):
            new = jnp.where(inside, 0.0, rows[i])
            entry = columns(rows[i], b)
            for j in range(8):
                new = new - entry[j] * solved[j]
            rows[i] = new
    return done


def basis_kernel(
    centred_ref, gram_ref, start_ref, masked_ref, loadings_ref, scores_ref, explained_ref,
    high_ref, low_ref, cov_high, cov_low, basis_ref, inverse_ref,
):
    var = lax.axis_index("var")
    samples = centred_ref.shape[0]
    local_vars = masked_ref.shape[0]
    width = local_vars * M
    high, low = split(centred_ref[...])
    high_ref[...] = high
    low_ref[...] = low
    cov = dot3((high, low), (high, low), TN) / (samples - 1)
    cov_high[...], cov_low[...] = split(cov)
    basis_ref[...] = start_ref[...]

    def sweep(_, carry):
        image = dot3((cov_high[...], cov_low[...]), split(basis_ref[...]), NN)
        gram = dot(image, image, TN, HIGHEST)
        for i, tile in enumerate(inverse_factor(gram)):
            inverse_ref[8 * i:8 * i + 8, :] = tile
        basis_ref[...] = dot(image, inverse_ref[...], NT, HIGHEST)
        return carry

    lax.fori_loop(0, SWEEPS, sweep, 0)

    scores = dot3((high_ref[...], low_ref[...]), split(basis_ref[...]), NN)
    scores_ref[...] = scores
    scores_low = scores.astype(BF16)
    own = pl.ds(pl.multiple_of(var * width, width), width)
    basis_low = basis_ref[own, :].astype(BF16)
    own_high, own_low = high_ref[:, own], low_ref[:, own]
    ones = jnp.ones((8, basis_low.shape[1]), F32)
    scores_wide = scores_low.astype(F32)
    for v in range(local_vars):
        mine = basis_low[v * M:(v + 1) * M, :]
        loadings_ref[v] = dot(mine, masked_ref[v], TN).astype(BF16)
        left, right = own_high[:, v * M:(v + 1) * M], own_low[:, v * M:(v + 1) * M]
        cross = dot(left, mine, NN) + dot(right, mine, NN)
        wide = mine.astype(F32)
        inner = dot(gram_ref[:, v * M:(v + 1) * M], wide, NN, HIGHEST)
        square = split(dot(wide, inner, TN, HIGHEST))
        quad = dot(scores_low, square[0], NN) + dot(scores_low, square[1], NN)
        gain = scores_wide * (2.0 * cross - quad)
        summed = dot(ones, gain, NT, HIGHEST) / M
        explained_ref[v:v + 1, :] = summed[0:1, :]


def finish(centred, gram, start, masked):
    local_vars, _, points = masked.shape
    samples, joint = centred.shape
    k = start.shape[1]
    return pl.pallas_call(
        basis_kernel,
        out_shape=(
            jax.ShapeDtypeStruct((local_vars, k, points), BF16),
            jax.ShapeDtypeStruct((samples, k), F32),
            jax.ShapeDtypeStruct((local_vars, samples), F32),
        ),
        in_specs=[pl.BlockSpec(memory_space=pltpu.VMEM)] * 4,
        out_specs=(pl.BlockSpec(memory_space=pltpu.VMEM),) * 3,
        scratch_shapes=[
            pltpu.VMEM((samples, joint), BF16),
            pltpu.VMEM((samples, joint), BF16),
            pltpu.VMEM((joint, joint), BF16),
            pltpu.VMEM((joint, joint), BF16),
            pltpu.VMEM((joint, k), F32),
            pltpu.VMEM((k, k), F32),
        ],
        compiler_params=pltpu.CompilerParams(vmem_limit_bytes=48 * 1024 * 1024),
        name="finish",
    )(centred, gram, start, masked)


def shards(n, nv, fields, eigenfunctions, start, grid_count):
    centred, gram, masked = gather_scores(n, nv, grid_count, fields, eigenfunctions)
    return finish(centred, gram, start, masked)


def solution(mesh):
    return jax.shard_map(
        functools.partial(shards, mesh.shape["space"], mesh.shape["var"]),
        mesh=mesh,
        in_specs=(P("var", None, "space"), P("var", None, "space"), P(), P()),
        out_specs=(P("var", None, "space"), P(), P("var", None)),
        check_vma=False,
    )
```

time: 61.9 us -> 49.1 us (0.79)
  Pallas kernels: 59.1 us -> 48.3 us
  local copies, waits for them, and re-layouts: 1.88 us -> 0.01 us
    pallas_call x1, Pallas kernels: 39 us -> 32 us  [gather_scores(): pl.pallas_call(functools.partial(gather_kernel, n, pieces), out_shape=(ja...]
    pallas_call x1, Pallas kernels: 20.1 us -> 16.3 us  [finish(): pl.pallas_call(basis_kernel, out_shape=(jax.ShapeDtypeStruct((local_vars,...]
    unnamed x6 -> x2, local copies, waits for them, and re-layouts: 1.88 us -> 0.01 us
where the time goes in v1:
time: 49.1 us; the launch traced here: 49 us
  Pallas kernels  48.3 us (98%)
  between operations  0.66 us (1%)
    pallas_call x1, Pallas kernels, gather_scores(): pl.pallas_call(functools.partial(gather_kernel, n, pieces), out_shape=(ja...  32 us
    pallas_call x1, Pallas kernels, finish(): pl.pallas_call(basis_kernel, out_shape=(jax.ShapeDtypeStruct((local_vars,...  16.3 us

profile of v1, /device:TPU:0, one launch (start us, length us, event | category | flops | bytes accessed | tf_op | source)
XLA Modules:
  0.0 49.0 jit_solution(4321867729020254102)
XLA Ops:
  0.6 0.0 copy-start
  0.6 32.0 %gather_scores.1 = (f32[1024,512]{1,0:T(8,128)S(1)}, f32[64,128]{1,0:T(8,128)S(1)}, bf16[2,64,4096]{2,1,0:T(8,128)(2,1)S(1)}) custom-call(s32[8]{0:T(128)} %counts_hbm.1, bf16[2,1024,4096]{2,1,0:T(8,128)(2,1)} %fields.1, bf16[2,64,4096]{2,1,0:T(8,128)(2,1)} %eigen_hbm.1), custom_call_target="tpu_custom_call" | custom-call | tf_op jit(solution)/shard_map/gather_scores/pallas_call | solution.py:273
  32.7 0.0 copy-done
  32.7 16.3 %finish.1 = (bf16[2,128,4096]{2,1,0:T(8,128)(2,1)}, f32[1024,128]{1,0:T(8,128)}, f32[2,1024]{1,0:T(2,128)}) custom-call(f32[1024,512]{1,0:T(8,128)S(1)} %get-tuple-element.6.centred_ref, f32[64,128]{1,0:T(8,128)S(1)} %get-tuple-element.7.gram_ref, f32[512,128]{1,0:T(8,128)S(1)} %copy-done, bf16[2,64,4096]{2,1,0:T(8,128)(2,1)S(1)} %get-tuple-element.8.masked_ref), custom_call_target="tpu_custom_call" | custom-call | tf_op jit(solution)/shard_map/finish/pallas_call | solution.py:428
Async XLA Ops:
  0.6 32.0 %copy-start = (f32[512,128]{1,0:T(8,128)S(1)}, f32[512,128]{1,0:T(8,128)}, u32[]{:S(2)}) copy-start(f32[512,128]{1,0:T(8,128)} %start_ref.1) | copy-start | bytes 786436

commit v2 on v1

--- a/solution.py
+++ b/solution.py
@@ -45,14 +45,27 @@
     return eigen * jnp.where(points < count, 1.0, 0.0).astype(eigen.dtype)
 
 
+SHARES = (4, 4, 4, 2, 2)
+AHEAD = 3
+
+
+def layout(samples):
+    unit = samples // (4 * sum(SHARES))
+    rows = [unit * share for share in SHARES]
+    return rows, [sum(rows[:p]) for p in range(len(rows))]
+
+
 def gather_kernel(
-    n, pieces, counts_hbm, fields, eigen_hbm, centred_ref, gram_ref, masked_ref,
-    counts, eigen, fbuf, weights, part, rbuf, cross, jbuf, gpart, grbuf, gred, gfull,
+    n, counts_hbm, fields, eigen_hbm, high_ref, low_ref, cov_high, cov_low, shift_ref, gram_ref, masked_ref,
+    counts, eigen, moment, fbuf, weights, part, rbuf, cross, jbuf, gpart, grbuf, gred, gfull,
     csem, esem, fsem, rsend, rrecv, xsend, xrecv, asend, arecv, psend, precv, gsend, grecv, hsend, hrecv,
 ):
     var, me = lax.axis_index("var"), lax.axis_index("space")
     local_vars, samples, local_points = fields.shape
-    rows = samples // (4 * pieces)
+    rows, start = layout(samples)
+    pieces = len(rows)
+    chunk = 2 * rows[0]
+    full = sum(size == rows[0] for size in rows)
     width = local_vars * M
     groups = n // 4
     side, core = var // 2, lax.rem(var, 2)
@@ -64,15 +77,17 @@
         return 2 * (depth + dz - 2 * depth * dz) + lane_y + dy - 2 * lane_y * dy
 
     def fetch(i):
-        first = (4 * (i // 2) + 2 * (owner(1 - lax.rem(i, 2), 0) // 2)) * rows
-        block = pl.ds(pl.multiple_of(first, 2 * rows), 2 * rows)
+        swapped = 2 * (i // 2) + lax.rem(depth + 1 + i, 2)
+        first = chunk * jnp.where(i < 2 * full, swapped, i)
+        block = pl.ds(pl.multiple_of(first, chunk), chunk)
         return pltpu.make_async_copy(fields.at[:, block, :], fbuf.at[i], fsem.at[i])
 
     eigen_copy = pltpu.make_async_copy(eigen_hbm, eigen, esem)
     counts_copy = pltpu.make_async_copy(counts_hbm, counts, csem)
     counts_copy.start()
     eigen_copy.start()
-    lax.fori_loop(0, 2 * pieces, lambda i, carry: (fetch(i).start(), carry)[1], 0)
+    for i in range(min(2, samples // chunk)):
+        fetch(i).start()
 
     xside, yside, zside = (2 * far + mate, me), (2 * side + mate, 4 * group + owner(0, 1)), (2 * side + mate, 4 * group + owner(1, 0))
     corner, partner = (2 * far + mate, 4 * group + owner(1, 1)), (2 * side + mate, me)
@@ -84,56 +99,74 @@
 
     counts_copy.wait()
     eigen_copy.wait()
+    for i in range(2, min(AHEAD, samples // chunk)):
+        fetch(i).start()
     for v in range(local_vars):
         masked = masked_block(counts[var * local_vars + v], eigen[v], me * local_points)
         masked_ref[v] = masked
-        weights[:, v * M:(v + 1) * M] = masked.T
+        weights[v * M:(v + 1) * M, :] = masked
 
     pl.semaphore_wait(barrier, n - 1 + 5)
 
+    def span(p, o):
+        return pl.ds(pl.multiple_of(4 * start[p] + o * rows[p], 8), rows[p])
+
     def send_part(p, k):
+        o = owner(1 - k // 2, 1 - k % 2)
+        if isinstance(p, int):
+            source = part.at[span(p, o)]
+            slot = rbuf.at[pl.ds(3 * start[p] + k * rows[p], rows[p])]
+        else:
+            source = part.at[pl.ds(pl.multiple_of((4 * p + o) * rows[0], 8), rows[0])]
+            slot = rbuf.at[pl.ds(pl.multiple_of((3 * p + k) * rows[0], 8), rows[0])]
         j = 3 * p + k
-        source = part.at[2 * p + k // 2, 1 - lane_y if k % 2 == 0 else lane_y]
-        target = (var, 4 * group + owner(1 - k // 2, 1 - k % 2))
-        return remote(source, rbuf.at[j], rsend.at[j], rrecv.at[j], target)
-
-    column = lax.broadcasted_iota(jnp.int32, (2 * rows, width), 1) // M
-
-    def project(i):
+        return remote(source, slot, rsend.at[j], rrecv.at[j], (var, 4 * group + o))
+
+    column = lax.broadcasted_iota(jnp.int32, (chunk, width), 1) // M
+
+    def project(i, first):
+        later = i + AHEAD
+        if not isinstance(i, int):
+            pl.when(later < samples // chunk)(lambda: fetch(later).start())
+        elif later < samples // chunk:
+            fetch(later).start()
         fetch(i).wait()
-        scores = dot(fbuf[i, 0], weights[...], NN)
+        scores = dot(fbuf[i, 0], weights[...], NT)
         for v in range(1, local_vars):
-            scores = jnp.where(column == v, dot(fbuf[i, v], weights[...], NN), scores)
-        part[i, 0] = scores[0:rows]
-        part[i, 1] = scores[rows:2 * rows]
+            scores = jnp.where(column == v, dot(fbuf[i, v], weights[...], NT), scores)
+        part[pl.ds(pl.multiple_of(first, chunk), chunk), :] = scores
 
     def step(p, carry):
         @pl.when(p > 0)
         def _():
             send_part(p - 1, 2).start()
 
-        project(2 * p)
+        project(2 * p, chunk * (2 * p + 1 - depth))
         send_part(p, 0).start()
         send_part(p, 1).start()
-        project(2 * p + 1)
+        project(2 * p + 1, chunk * (2 * p + depth))
         return carry
 
     def block(p, origin, o):
-        return jbuf.at[origin, pl.ds(pl.multiple_of((4 * p + o) * rows, rows), rows)]
+        return jbuf.at[origin, span(p, o)]
 
     own = [block(p, var, quad) for p in range(pieces)]
+
+    def held(p):
+        return pl.ds(start[p], rows[p])
 
     def send_cross(p, d):
         j = p * (groups - 1) + d - 1
         target = (var, 4 * lax.rem(group + d, groups) + quad)
-        return remote(cross.at[p, group], cross.at[p, group], xsend.at[j], xrecv.at[j], target)
+        return remote(cross.at[group, held(p)], cross.at[group, held(p)], xsend.at[j], xrecv.at[j], target)
 
     def half_sum(p):
-        total = part[2 * p + 1, lane_y]
+        total = part[span(p, quad), :]
         for k in range(3):
             send_part(p, k).wait_recv()
-            total = total + rbuf[3 * p + k]
-        cross[p, group] = total
+            first = 3 * start[p] + k * rows[p]
+            total = total + rbuf[first:first + rows[p], :]
+        cross[group, held(p)] = total
         for d in range(1, groups):
             send_cross(p, d).start()
 
@@ -151,12 +184,10 @@
     kinds = ("x", "y", "z", "xy", "xz", "yz", "xyz")
 
     def route(p, kind):
-        last = (("xyz", "yz", xside), ("xyz", "xz", yside), ("xyz", "xy", zside))[p % 3]
-        if p == pieces - 1:
-            last = ("xyz", "", corner)
+        last = ("yz", xside) if p == 0 else ("", corner)
         return {
             "x": ("", xside), "y": ("", yside), "z": ("", zside),
-            "xz": ("x", zside), "xy": ("y", xside), "yz": ("z", yside), "xyz": last[1:],
+            "xz": ("x", zside), "xy": ("y", xside), "yz": ("z", yside), "xyz": last,
         }[kind]
 
     def send_on(p, kind):
@@ -180,9 +211,9 @@
     def full_sum(p):
         for d in range(1, groups):
             send_cross(p, d).wait_recv()
-        total = cross[p, 0]
+        total = cross[0, held(p)]
         for g in range(1, groups):
-            total = total + cross[p, g]
+            total = total + cross[g, held(p)]
         own[p][...] = total
         for kind in kinds:
             if route(p, kind)[0] == "":
@@ -199,6 +230,23 @@
 
     def third_hop(p):
         arrived(p, "xyz")
+
+    def moments(first, last, initial):
+        for p in range(first, last + 1):
+            for kind in kinds + ("",):
+                share(p, kind).wait_recv()
+        place = slice(4 * start[first], 4 * (start[last] + rows[last]))
+        block = jnp.concatenate([jbuf[v, place, :] for v in range(jbuf.shape[0])], axis=1)
+        if initial:
+            shift_ref[0:1, :] = jnp.sum(block, axis=0, keepdims=True) / block.shape[0]
+        block = block - shift_ref[0:1, :]
+        total = jnp.sum(block, axis=0, keepdims=True)
+        high, low = split(block)
+        high_ref[place, :] = high
+        low_ref[place, :] = low
+        square = dot3((high, low), (high, low), TN)
+        shift_ref[1:2, :] = total if initial else shift_ref[1:2, :] + total
+        moment[...] = square if initial else moment[...] + square
 
     grows = M // n
 
@@ -228,18 +276,27 @@
         for d in range(1, n):
             send_gfull(d).start()
 
-    stages = (half_sum, full_sum, first_hop, second_hop, third_hop)
-    early = max(pieces - 1, 1)
-    lax.fori_loop(0, early, step, 0)
+    lax.fori_loop(0, full, step, 0)
+    send_part(full - 1, 2).start()
     half_sum(0)
-    lax.fori_loop(early, pieces, step, 0)
-    send_part(pieces - 1, 2).start()
+    for p in range(full, pieces):
+        project(full + p, chunk * (full + p))
+        for k in range(3):
+            send_part(p, k).start()
     gram_parts()
-    slots = sorted((1.5 * p + (0, 2.2, 3.8, 5.4, 7.0)[s], s, p) for s in range(5) for p in range(pieces))
-    for at, s, p in slots[1:]:
-        if (s, p) == (2, pieces - 1):
+    order = (
+        (0, 1), (0, 2), (0, 3), (1, 0), (0, 4), (1, 1), (2, 0), (1, 2), (1, 3), (1, 4), (5, 0), (2, 1), (3, 0),
+        (2, 2), (2, 3), (2, 4), (3, 1), (4, 1), (4, 0), (3, 2), (4, 2), (3, 3), (4, 3), (3, 4), (4, 4),
+    )
+    for stage, p in order:
+        if stage == 5:
             gram_sum()
-        stages[s](p)
+        else:
+            (half_sum, full_sum, first_hop, second_hop, third_hop)[stage](p)
+    moments(1, 1, True)
+    moments(0, 0, False)
+    moments(2, 2, False)
+    moments(3, 4, False)
 
     for d in range(1, n):
         send_gfull(d).wait()
@@ -251,42 +308,52 @@
         for kind in kinds:
             send_on(p, kind).wait_send()
         for kind in kinds + ("",):
-            share(p, kind).wait()
-
-    for v in range(2 * (jbuf.shape[0] // 2)):
-        mean = jnp.sum(jbuf[v], axis=0, keepdims=True) / samples
-        centred_ref[:, v * width:(v + 1) * width] = jbuf[v] - mean
+            share(p, kind).wait_send()
+
+    offset = shift_ref[1:2, :] / samples
+    shift_ref[0:1, :] = offset
+    tall = jnp.where(lax.broadcasted_iota(jnp.int32, (16, offset.shape[1]), 0) == 0, offset, 0.0)
+    outer = split(tall)
+    cov = (moment[...] - samples * dot3(outer, outer, TN)) / (samples - 1)
+    cov_high[...], cov_low[...] = split(cov)
     for s in range(n):
         gram_ref[s * grows:(s + 1) * grows, :] = gfull[s, 0:grows, :]
 
 
 def gather_scores(n, nv, counts, fields, eigen):
     local_vars, samples, points = fields.shape
-    pieces = 4
-    if nv != 4 or n % 4 or samples % (4 * pieces):
+    rows, _ = layout(samples)
+    pieces = len(rows)
+    if nv != 4 or n % 4 or samples % (64 * sum(SHARES)):
         raise ValueError("unsupported mesh")
-    rows = samples // (4 * pieces)
+    chunk = 2 * rows[0]
+    quarter = samples // 4
     width = local_vars * M
     groups = n // 4
     dma = pltpu.SemaphoreType.DMA
     pairs = [3 * pieces, max(1, pieces * (groups - 1)), 7 * pieces, 8 * pieces, n - 1, n - 1]
     return pl.pallas_call(
-        functools.partial(gather_kernel, n, pieces),
+        functools.partial(gather_kernel, n),
         out_shape=(
-            jax.ShapeDtypeStruct((samples, nv * width), F32),
+            jax.ShapeDtypeStruct((samples, nv * width), BF16),
+            jax.ShapeDtypeStruct((samples, nv * width), BF16),
+            jax.ShapeDtypeStruct((nv * width, nv * width), BF16),
+            jax.ShapeDtypeStruct((nv * width, nv * width), BF16),
+            jax.ShapeDtypeStruct((8, nv * width), F32),
             jax.ShapeDtypeStruct((M, width), F32),
             jax.ShapeDtypeStruct((local_vars, M, points), BF16),
         ),
         in_specs=[pl.BlockSpec(memory_space=pltpu.HBM)] * 3,
-        out_specs=(pl.BlockSpec(memory_space=pltpu.VMEM),) * 3,
+        out_specs=(pl.BlockSpec(memory_space=pltpu.VMEM),) * 7,
         scratch_shapes=[
             pltpu.SMEM(counts.shape, jnp.int32),
             pltpu.VMEM((local_vars, M, points), BF16),
-            pltpu.VMEM((2 * pieces, local_vars, 2 * rows, points), BF16),
-            pltpu.VMEM((points, width), BF16),
-            pltpu.VMEM((2 * pieces, 2, rows, width), F32),
-            pltpu.VMEM((3 * pieces, rows, width), F32),
-            pltpu.VMEM((pieces, groups, rows, width), F32),
+            pltpu.VMEM((nv * width, nv * width), F32),
+            pltpu.VMEM((samples // chunk, local_vars, chunk, points), BF16),
+            pltpu.VMEM((width, points), BF16),
+            pltpu.VMEM((samples, width), F32),
+            pltpu.VMEM((3 * quarter, width), F32),
+            pltpu.VMEM((groups, quarter, width), F32),
             pltpu.VMEM((nv, samples, width), F32),
             pltpu.VMEM((n, 8, width), F32),
             pltpu.VMEM((n - 1, 8, width), F32),
@@ -294,7 +361,7 @@
             pltpu.VMEM((n, 8, width), F32),
             dma(()),
             dma(()),
-            dma((2 * pieces,)),
+            dma((samples // chunk,)),
             *[dma((count,)) for count in pairs for _ in range(2)],
         ],
         compiler_params=pltpu.CompilerParams(
@@ -374,23 +441,25 @@
     return done
 
 
+def packed(left, right):
+    (lh, ll), (rh, rl) = left, right
+    k = rh.shape[1]
+    both = dot(lh, jnp.concatenate([rh, rl], axis=1), NN)
+    return both[:, 0:k] + (both[:, k:2 * k] + dot(ll, rh, NN))
+
+
 def basis_kernel(
-    centred_ref, gram_ref, start_ref, masked_ref, loadings_ref, scores_ref, explained_ref,
-    high_ref, low_ref, cov_high, cov_low, basis_ref, inverse_ref,
+    high_ref, low_ref, cov_high, cov_low, shift_ref, gram_ref, start_ref, masked_ref,
+    loadings_hbm, scores_hbm, explained_ref, loadings_ref, scores_ref, basis_ref, inverse_ref, lsem, ssem,
 ):
     var = lax.axis_index("var")
-    samples = centred_ref.shape[0]
     local_vars = masked_ref.shape[0]
     width = local_vars * M
-    high, low = split(centred_ref[...])
-    high_ref[...] = high
-    low_ref[...] = low
-    cov = dot3((high, low), (high, low), TN) / (samples - 1)
-    cov_high[...], cov_low[...] = split(cov)
+    k = start_ref.shape[1]
     basis_ref[...] = start_ref[...]
 
     def sweep(_, carry):
-        image = dot3((cov_high[...], cov_low[...]), split(basis_ref[...]), NN)
+        image = packed((cov_high[...], cov_low[...]), split(basis_ref[...]))
         gram = dot(image, image, TN, HIGHEST)
         for i, tile in enumerate(inverse_factor(gram)):
             inverse_ref[8 * i:8 * i + 8, :] = tile
@@ -399,31 +468,50 @@
 
     lax.fori_loop(0, SWEEPS, sweep, 0)
 
-    scores = dot3((high_ref[...], low_ref[...]), split(basis_ref[...]), NN)
-    scores_ref[...] = scores
-    scores_low = scores.astype(BF16)
     own = pl.ds(pl.multiple_of(var * width, width), width)
     basis_low = basis_ref[own, :].astype(BF16)
-    own_high, own_low = high_ref[:, own], low_ref[:, own]
-    ones = jnp.ones((8, basis_low.shape[1]), F32)
+    mine = [basis_low[v * M:(v + 1) * M, :] for v in range(local_vars)]
+    flush = []
+    for v in range(local_vars):
+        loadings_ref[v] = dot(mine[v], masked_ref[v], TN).astype(BF16)
+        flush.append(pltpu.make_async_copy(loadings_ref.at[v], loadings_hbm.at[v], lsem.at[v]))
+        flush[v].start()
+
+    offset = shift_ref[0:1, :]
+    tall = jnp.where(lax.broadcasted_iota(jnp.int32, (8, offset.shape[1]), 0) == 0, offset, 0.0)
+    scores = packed((high_ref[...], low_ref[...]), split(basis_ref[...])) - dot(tall, basis_ref[...], NN, HIGHEST)[0:1, :]
+    scores_ref[...] = scores
+    flush.append(pltpu.make_async_copy(scores_ref, scores_hbm, ssem))
+    flush[-1].start()
+
+    scores_low = scores.astype(BF16)
+    wide = basis_low.astype(F32)
+    zero = jnp.zeros((M, k), F32)
+    spread, quads = [], []
+    for v in range(local_vars):
+        line = wide[v * M:(v + 1) * M, :]
+        spread.append(jnp.concatenate([2.0 * line if u == v else zero for u in range(local_vars)], axis=1))
+        inner = dot(gram_ref[:, v * M:(v + 1) * M], line, NN, HIGHEST)
+        quads.append(dot(line, inner, TN, HIGHEST))
+    cross = jnp.concatenate(spread, axis=0)
+    square = split(-jnp.concatenate(quads, axis=1))
+    right = jnp.concatenate([cross.astype(BF16), cross.astype(BF16), square[0], square[1]], axis=0)
+    left = jnp.concatenate([high_ref[:, own], low_ref[:, own], scores_low, scores_low], axis=1)
+    tall = jnp.where(lax.broadcasted_iota(jnp.int32, (8, width), 0) == 0, shift_ref[0:1, own], 0.0)
+    inside = dot(left, right, NN) - dot(tall, cross, NN, HIGHEST)[0:1, :]
+    ones = jnp.ones((16, k), BF16)
     scores_wide = scores_low.astype(F32)
     for v in range(local_vars):
-        mine = basis_low[v * M:(v + 1) * M, :]
-        loadings_ref[v] = dot(mine, masked_ref[v], TN).astype(BF16)
-        left, right = own_high[:, v * M:(v + 1) * M], own_low[:, v * M:(v + 1) * M]
-        cross = dot(left, mine, NN) + dot(right, mine, NN)
-        wide = mine.astype(F32)
-        inner = dot(gram_ref[:, v * M:(v + 1) * M], wide, NN, HIGHEST)
-        square = split(dot(wide, inner, TN, HIGHEST))
-        quad = dot(scores_low, square[0], NN) + dot(scores_low, square[1], NN)
-        gain = scores_wide * (2.0 * cross - quad)
-        summed = dot(ones, gain, NT, HIGHEST) / M
+        gain = split(scores_wide * inside[:, v * k:(v + 1) * k])
+        summed = (dot(ones, gain[0], NT) + dot(ones, gain[1], NT)) / M
         explained_ref[v:v + 1, :] = summed[0:1, :]
-
-
-def finish(centred, gram, start, masked):
+    for copy in flush:
+        copy.wait()
+
+
+def finish(high, low, cov_high, cov_low, shift, gram, start, masked):
     local_vars, _, points = masked.shape
-    samples, joint = centred.shape
+    samples, joint = high.shape
     k = start.shape[1]
     return pl.pallas_call(
         basis_kernel,
@@ -432,24 +520,28 @@
             jax.ShapeDtypeStruct((samples, k), F32),
             jax.ShapeDtypeStruct((local_vars, samples), F32),
         ),
-        in_specs=[pl.BlockSpec(memory_space=pltpu.VMEM)] * 4,
-        out_specs=(pl.BlockSpec(memory_space=pltpu.VMEM),) * 3,
+        in_specs=[pl.BlockSpec(memory_space=pltpu.VMEM)] * 8,
+        out_specs=(
+            pl.BlockSpec(memory_space=pltpu.HBM),
+            pl.BlockSpec(memory_space=pltpu.HBM),
+            pl.BlockSpec(memory_space=pltpu.VMEM),
+        ),
         scratch_shapes=[
-            pltpu.VMEM((samples, joint), BF16),
-            pltpu.VMEM((samples, joint), BF16),
-            pltpu.VMEM((joint, joint), BF16),
-            pltpu.VMEM((joint, joint), BF16),
+            pltpu.VMEM((local_vars, k, points), BF16),
+            pltpu.VMEM((samples, k), F32),
             pltpu.VMEM((joint, k), F32),
             pltpu.VMEM((k, k), F32),
+            pltpu.SemaphoreType.DMA((local_vars,)),
+            pltpu.SemaphoreType.DMA(()),
         ],
         compiler_params=pltpu.CompilerParams(vmem_limit_bytes=48 * 1024 * 1024),
         name="finish",
-    )(centred, gram, start, masked)
+    )(high, low, cov_high, cov_low, shift, gram, start, masked)
 
 
 def shards(n, nv, fields, eigenfunctions, start, grid_count):
-    centred, gram, masked = gather_scores(n, nv, grid_count, fields, eigenfunctions)
-    return finish(centred, gram, start, masked)
+    high, low, cov_high, cov_low, shift, gram, masked = gather_scores(n, nv, grid_count, fields, eigenfunctions)
+    return finish(high, low, cov_high, cov_low, shift, gram, start, masked)
 
 
 def solution(mesh):

time: 49.1 us -> 45.8 us (0.933)
  Pallas kernels: 48.3 us -> 44.8 us
    pallas_call x1, Pallas kernels: 16.3 us -> 12.2 us  [finish(): pl.pallas_call(basis_kernel, out_shape=(jax.ShapeDtypeStruct((local_vars,...]
    pallas_call x1, Pallas kernels: 32 us -> 32.6 us  [gather_scores(): pl.pallas_call(functools.partial(gather_kernel, n), out_shape=(jax.ShapeD...]
where the time goes in v2:
time: 45.8 us; the launch traced here: 45.5 us
  Pallas kernels  44.8 us (98%)
  between operations  0.65 us (1%)
    pallas_call x1, Pallas kernels, gather_scores(): pl.pallas_call(functools.partial(gather_kernel, n), out_shape=(jax.ShapeD...  32.6 us
    pallas_call x1, Pallas kernels, finish(): pl.pallas_call(basis_kernel, out_shape=(jax.ShapeDtypeStruct((local_vars,...  12.2 us

profile of v2, /device:TPU:0, one launch (start us, length us, event | category | flops | bytes accessed | tf_op | source)
XLA Modules:
  0.0 45.5 jit_solution(3688361242716169406)
XLA Ops:
  0.6 0.0 copy-start
  0.6 32.6 %gather_scores.1 = (bf16[1024,512]{1,0:T(8,128)(2,1)S(1)}, bf16[1024,512]{1,0:T(8,128)(2,1)S(1)}, bf16[512,512]{1,0:T(8,128)(2,1)S(1)}, bf16[512,512]{1,0:T(8,12...) custom-call(s32[8]{0:T(128)} %counts_hbm.1, ...), custom_call_target="tpu_custom_call" | custom-call | tf_op jit(solution)/shard_map/gather_scores/pallas_call | solution.py:335
  33.2 0.0 copy-done
  33.2 12.2 %finish.1 = (bf16[2,128,4096]{2,1,0:T(8,128)(2,1)}, f32[1024,128]{1,0:T(8,128)}, f32[2,1024]{1,0:T(2,128)}) custom-call(bf16[1024,512]{1,0:T(8,128)(2,1)S(1)} %get-tuple-element.10.high_ref, bf16[1024,512]{1,0:T(8,128)(2,1)S(1)} %get-tuple-element.11.low_ref, bf16[512,512]{1,0:T(8,128)(2,1)S(1)} %get-tuple-element.12.cov_high, ...), custom_call_target="tpu_custom_call" | custom-call | tf_op jit(solution)/shard_map/finish/pallas_call | solution.py:516
Async XLA Ops:
  0.6 32.6 %copy-start = (f32[512,128]{1,0:T(8,128)S(1)}, f32[512,128]{1,0:T(8,128)}, u32[]{:S(2)}) copy-start(f32[512,128]{1,0:T(8,128)} %start_ref.1) | copy-start | bytes 786436

commit v3 on v2

--- a/solution.py
+++ b/solution.py
@@ -46,7 +46,7 @@
 
 
 SHARES = (4, 4, 4, 2, 2)
-AHEAD = 3
+AHEAD = 4
 
 
 def layout(samples):
@@ -285,7 +285,7 @@
             send_part(p, k).start()
     gram_parts()
     order = (
-        (0, 1), (0, 2), (0, 3), (1, 0), (0, 4), (1, 1), (2, 0), (1, 2), (1, 3), (1, 4), (5, 0), (2, 1), (3, 0),
+        (0, 1), (0, 2), (0, 3), (0, 4), (1, 0), (1, 1), (2, 0), (1, 2), (1, 3), (1, 4), (5, 0), (2, 1), (3, 0),
         (2, 2), (2, 3), (2, 4), (3, 1), (4, 1), (4, 0), (3, 2), (4, 2), (3, 3), (4, 3), (3, 4), (4, 4),
     )
     for stage, p in order:
@@ -384,9 +384,17 @@
     def spread(tile, j):
         return jnp.broadcast_to(tile[j:j + 1, :], (8, size))
 
-    done = []
+    done, top = [], []
+    half = tiles // 2
     block = columns(rows[0], 0)
     for b in range(tiles):
+        limit = half if b < half else tiles
+        if b == half:
+            upper = jnp.concatenate(top, axis=0)
+            update = dot(upper[:, 8 * half:], upper, TN, HIGHEST)
+            for i in range(half, tiles):
+                rows[i] = jnp.where(lane < 8 * half, 0.0, rows[i]) - update[8 * (i - half):8 * (i - half) + 8, :]
+            block = columns(rows[b], b)
         inside = (lane >= 8 * b) & (lane < 8 * b + 8)
         work = jnp.where(inside, jnp.where(lane - 8 * b == sublane, 1.0, 0.0), rows[b])
         inverse, cross, lower = [], {}, []
@@ -405,11 +413,13 @@
             for q in range(j + 2, 8):
                 block[q] = block[q] - factor * cross[j, q]
             work = work - jnp.where(sublane > j, factor, 0.0) * spread(work, j)
-        done.append(jnp.where(lane < 8 * b + 8, work, 0.0) * lax.rsqrt(pivot))
-        if b + 1 == tiles:
-            break
+        scaled = work * lax.rsqrt(pivot)
+        top.append(jnp.where((lane < 8 * b + 8) | (lane >= 8 * half), scaled, 0.0))
+        done.append(jnp.where(lane < 8 * b + 8, scaled, 0.0))
+        if b + 1 == limit:
+            continue
         line = [spread(work, j) for j in range(8)]
-        for i in range(b + 1, min(b + 3, tiles)):
+        for i in range(b + 1, min(b + 3, limit)):
             value, factors = columns(rows[i], b), []
             for j in range(8):
                 factors.append(value[j] * inverse[j])
@@ -424,7 +434,7 @@
             for j in range(8):
                 new = new - factors[j] * line[j]
             rows[i] = new
-        if b + 3 >= tiles:
+        if b + 3 >= limit:
             continue
         solved = [None] * 8
         for j in reversed(range(8)):
@@ -432,20 +442,13 @@
             for q in range(j + 1, 8):
                 value = value - spread(lower[j], q) * solved[q]
             solved[j] = value
-        for i in range(b + 3, tiles):
+        for i in range(b + 3, limit):
             new = jnp.where(inside, 0.0, rows[i])
             entry = columns(rows[i], b)
             for j in range(8):
                 new = new - entry[j] * solved[j]
             rows[i] = new
     return done
-
-
-def packed(left, right):
-    (lh, ll), (rh, rl) = left, right
-    k = rh.shape[1]
-    both = dot(lh, jnp.concatenate([rh, rl], axis=1), NN)
-    return both[:, 0:k] + (both[:, k:2 * k] + dot(ll, rh, NN))
 
 
 def basis_kernel(
@@ -456,49 +459,53 @@
     local_vars = masked_ref.shape[0]
     width = local_vars * M
     k = start_ref.shape[1]
-    basis_ref[...] = start_ref[...]
+    basis_ref[...] = start_ref[...].T
 
     def sweep(_, carry):
-        image = packed((cov_high[...], cov_low[...]), split(basis_ref[...]))
-        gram = dot(image, image, TN, HIGHEST)
+        high, low = split(basis_ref[...])
+        both = dot(jnp.concatenate([high, low], axis=0), cov_high[...], NN)
+        image = both[0:k] + (both[k:2 * k] + dot(high, cov_low[...], NN))
+        gram = dot(image, image, NT, HIGHEST)
         for i, tile in enumerate(inverse_factor(gram)):
             inverse_ref[8 * i:8 * i + 8, :] = tile
-        basis_ref[...] = dot(image, inverse_ref[...], NT, HIGHEST)
+        basis_ref[...] = dot(inverse_ref[...], image, NN, HIGHEST)
         return carry
 
     lax.fori_loop(0, SWEEPS, sweep, 0)
 
     own = pl.ds(pl.multiple_of(var * width, width), width)
-    basis_low = basis_ref[own, :].astype(BF16)
-    mine = [basis_low[v * M:(v + 1) * M, :] for v in range(local_vars)]
+    mine = basis_ref[:, own].astype(BF16)
     flush = []
     for v in range(local_vars):
-        loadings_ref[v] = dot(mine[v], masked_ref[v], TN).astype(BF16)
+        loadings_ref[v] = dot(mine[:, v * M:(v + 1) * M], masked_ref[v], NN).astype(BF16)
         flush.append(pltpu.make_async_copy(loadings_ref.at[v], loadings_hbm.at[v], lsem.at[v]))
         flush[v].start()
 
+    high, low = split(basis_ref[...])
     offset = shift_ref[0:1, :]
     tall = jnp.where(lax.broadcasted_iota(jnp.int32, (8, offset.shape[1]), 0) == 0, offset, 0.0)
-    scores = packed((high_ref[...], low_ref[...]), split(basis_ref[...])) - dot(tall, basis_ref[...], NN, HIGHEST)[0:1, :]
+    both = dot(high_ref[...], jnp.concatenate([high, low], axis=0), NT)
+    mean = dot(tall, basis_ref[...], NT, HIGHEST)[0:1, :]
+    scores = both[:, 0:k] + (both[:, k:2 * k] + dot(low_ref[...], high, NT)) - mean
     scores_ref[...] = scores
     flush.append(pltpu.make_async_copy(scores_ref, scores_hbm, ssem))
     flush[-1].start()
 
     scores_low = scores.astype(BF16)
-    wide = basis_low.astype(F32)
-    zero = jnp.zeros((M, k), F32)
+    wide = mine.astype(F32)
+    owner = lax.broadcasted_iota(jnp.int32, (k, width), 1) // M
     spread, quads = [], []
     for v in range(local_vars):
-        line = wide[v * M:(v + 1) * M, :]
-        spread.append(jnp.concatenate([2.0 * line if u == v else zero for u in range(local_vars)], axis=1))
-        inner = dot(gram_ref[:, v * M:(v + 1) * M], line, NN, HIGHEST)
-        quads.append(dot(line, inner, TN, HIGHEST))
+        line = wide[:, v * M:(v + 1) * M]
+        spread.append(jnp.where(owner == v, 2.0 * wide, 0.0))
+        inner = dot(line, gram_ref[:, v * M:(v + 1) * M], NN, HIGHEST)
+        quads.append(dot(inner, line, NT, HIGHEST))
     cross = jnp.concatenate(spread, axis=0)
-    square = split(-jnp.concatenate(quads, axis=1))
-    right = jnp.concatenate([cross.astype(BF16), cross.astype(BF16), square[0], square[1]], axis=0)
+    square = split(-jnp.concatenate(quads, axis=0))
+    right = jnp.concatenate([cross.astype(BF16), cross.astype(BF16), square[0], square[1]], axis=1)
     left = jnp.concatenate([high_ref[:, own], low_ref[:, own], scores_low, scores_low], axis=1)
     tall = jnp.where(lax.broadcasted_iota(jnp.int32, (8, width), 0) == 0, shift_ref[0:1, own], 0.0)
-    inside = dot(left, right, NN) - dot(tall, cross, NN, HIGHEST)[0:1, :]
+    inside = dot(left, right, NT) - dot(tall, cross, NT, HIGHEST)[0:1, :]
     ones = jnp.ones((16, k), BF16)
     scores_wide = scores_low.astype(F32)
     for v in range(local_vars):
@@ -529,7 +536,7 @@
         scratch_shapes=[
             pltpu.VMEM((local_vars, k, points), BF16),
             pltpu.VMEM((samples, k), F32),
-            pltpu.VMEM((joint, k), F32),
+            pltpu.VMEM((k, joint), F32),
             pltpu.VMEM((k, k), F32),
             pltpu.SemaphoreType.DMA((local_vars,)),
             pltpu.SemaphoreType.DMA(()),

time: 45.8 us -> 45.6 us (level)
    pallas_call x1, Pallas kernels: 12.2 us -> 11.8 us  [finish(): pl.pallas_call(basis_kernel, out_shape=(jax.ShapeDtypeStruct((local_vars,...]
where the time goes in v3:
time: 45.6 us; the launch traced here: 45.4 us
  Pallas kernels  44.8 us (98%)
  between operations  0.65 us (1%)
    pallas_call x1, Pallas kernels, gather_scores(): pl.pallas_call(functools.partial(gather_kernel, n), out_shape=(jax.ShapeD...  33 us
    pallas_call x1, Pallas kernels, finish(): pl.pallas_call(basis_kernel, out_shape=(jax.ShapeDtypeStruct((local_vars,...  11.8 us

profile of v3, /device:TPU:0, one launch (start us, length us, event | category | flops | bytes accessed | tf_op | source)
XLA Modules:
  0.0 45.4 jit_solution(7664144580916609084)
XLA Ops:
  0.6 0.0 copy-start
  0.6 33.0 %gather_scores.1 = (bf16[1024,512]{1,0:T(8,128)(2,1)S(1)}, bf16[1024,512]{1,0:T(8,128)(2,1)S(1)}, bf16[512,512]{1,0:T(8,128)(2,1)S(1)}, bf16[512,512]{1,0:T(8,12...) custom-call(s32[8]{0:T(128)} %counts_hbm.1, ...), custom_call_target="tpu_custom_call" | custom-call | tf_op jit(solution)/shard_map/gather_scores/pallas_call | solution.py:335
  33.7 0.0 copy-done
  33.7 11.8 %finish.1 = (bf16[2,128,4096]{2,1,0:T(8,128)(2,1)}, f32[1024,128]{1,0:T(8,128)}, f32[2,1024]{1,0:T(2,128)}) custom-call(bf16[1024,512]{1,0:T(8,128)(2,1)S(1)} %get-tuple-element.10.high_ref, bf16[1024,512]{1,0:T(8,128)(2,1)S(1)} %get-tuple-element.11.low_ref, bf16[512,512]{1,0:T(8,128)(2,1)S(1)} %get-tuple-element.12.cov_high, ...), custom_call_target="tpu_custom_call" | custom-call | tf_op jit(solution)/shard_map/finish/pallas_call | solution.py:523
Async XLA Ops:
  0.6 33.0 %copy-start = (f32[512,128]{1,0:T(8,128)S(1)}, f32[512,128]{1,0:T(8,128)}, u32[]{:S(2)}) copy-start(f32[512,128]{1,0:T(8,128)} %start_ref.1) | copy-start | bytes 786436

commit v4 on v3

--- a/solution.py
+++ b/solution.py
@@ -215,7 +215,7 @@
         for g in range(1, groups):
             total = total + cross[g, held(p)]
         own[p][...] = total
-        for kind in kinds:
+        for kind in reversed(kinds):
             if route(p, kind)[0] == "":
                 send_on(p, kind).start()
         share(p, "").start()
@@ -283,14 +283,13 @@
         project(full + p, chunk * (full + p))
         for k in range(3):
             send_part(p, k).start()
-    gram_parts()
     order = (
-        (0, 1), (0, 2), (0, 3), (0, 4), (1, 0), (1, 1), (2, 0), (1, 2), (1, 3), (1, 4), (5, 0), (2, 1), (3, 0),
+        (0, 1), (0, 2), (5, 1), (0, 3), (0, 4), (1, 0), (1, 1), (2, 0), (1, 2), (1, 3), (1, 4), (5, 0), (2, 1), (3, 0),
         (2, 2), (2, 3), (2, 4), (3, 1), (4, 1), (4, 0), (3, 2), (4, 2), (3, 3), (4, 3), (3, 4), (4, 4),
     )
     for stage, p in order:
         if stage == 5:
-            gram_sum()
+            (gram_parts if p == 1 else gram_sum)()
         else:
             (half_sum, full_sum, first_hop, second_hop, third_hop)[stage](p)
     moments(1, 1, True)

time: 45.6 us -> 44.7 us (0.980)
  Pallas kernels: 44.8 us -> 43.6 us
    pallas_call x1, Pallas kernels: 33 us -> 31.9 us  [gather_scores(): pl.pallas_call(functools.partial(gather_kernel, n), out_shape=(jax.ShapeD...]
where the time goes in v4:
time: 44.7 us; the launch traced here: 44.3 us
  Pallas kernels  43.6 us (98%)
  between operations  0.65 us (1%)
    pallas_call x1, Pallas kernels, gather_scores(): pl.pallas_call(functools.partial(gather_kernel, n), out_shape=(jax.ShapeD...  31.9 us
    pallas_call x1, Pallas kernels, finish(): pl.pallas_call(basis_kernel, out_shape=(jax.ShapeDtypeStruct((local_vars,...  11.8 us

profile of v4, /device:TPU:0, one launch (start us, length us, event | category | flops | bytes accessed | tf_op | source)
XLA Modules:
  0.0 44.3 jit_solution(4758883527166011678)
XLA Ops:
  0.6 0.0 copy-start
  0.6 31.9 %gather_scores.1 = (bf16[1024,512]{1,0:T(8,128)(2,1)S(1)}, bf16[1024,512]{1,0:T(8,128)(2,1)S(1)}, bf16[512,512]{1,0:T(8,128)(2,1)S(1)}, bf16[512,512]{1,0:T(8,12...) custom-call(s32[8]{0:T(128)} %counts_hbm.1, ...), custom_call_target="tpu_custom_call" | custom-call | tf_op jit(solution)/shard_map/gather_scores/pallas_call | solution.py:334
  32.5 0.0 copy-done
  32.5 11.8 %finish.1 = (bf16[2,128,4096]{2,1,0:T(8,128)(2,1)}, f32[1024,128]{1,0:T(8,128)}, f32[2,1024]{1,0:T(2,128)}) custom-call(bf16[1024,512]{1,0:T(8,128)(2,1)S(1)} %get-tuple-element.10.high_ref, bf16[1024,512]{1,0:T(8,128)(2,1)S(1)} %get-tuple-element.11.low_ref, bf16[512,512]{1,0:T(8,128)(2,1)S(1)} %get-tuple-element.12.cov_high, ...), custom_call_target="tpu_custom_call" | custom-call | tf_op jit(solution)/shard_map/finish/pallas_call | solution.py:522
Async XLA Ops:
  0.6 31.9 %copy-start = (f32[512,128]{1,0:T(8,128)S(1)}, f32[512,128]{1,0:T(8,128)}, u32[]{:S(2)}) copy-start(f32[512,128]{1,0:T(8,128)} %start_ref.1) | copy-start | bytes 786436
